TPU v7x, 256 devices: a whole 4x4x8 slice. The times are simulated.
256 devices in a mesh: group: 16 (over z, x_hi), expert: 16 (over x_lo, y, core).
Axes of the slice: x: 4 (x_hi: 2, x_lo: 2; x = x_hi * 2 + x_lo), y: 4, z: 8, core: 2. Of those that a mesh axis runs over, the one named last changes fastest.
Arguments:
- hidden_in: bfloat16 [16384, 2048], P(('group', 'expert')), may hold values from -54 to 54
- norm_attention: float32 [2048], replicated, may hold values from 0.5 to 1.5
- norm_experts: float32 [2048], replicated, may hold values from 0.5 to 1.5
- query_master: float32 [2048, 4096], P('group', 'expert'), may hold values from -0.125 to 0.125
- trainer_key_value_weight: float32 [2, 2048, 512], P(None, 'group'), may hold values from -0.125 to 0.125
- output_master: float32 [4096, 2048], P('expert', 'group'), may hold values from -0.09375 to 0.09375
- query_gain: float32 [128], replicated, may hold values from 0.5 to 1.5
- key_gain: float32 [128], replicated, may hold values from 0.5 to 1.5
- lengths: int32 [8], replicated, may hold values from 1 to 2048, as said below
- router: bfloat16 [2048, 128], replicated, may hold values from -0.125 to 0.125
- expert_gateup: bfloat16 [16, 2048, 1536], P('expert'), may hold values from -0.125 to 0.125
- expert_down: bfloat16 [16, 768, 2048], P('expert'), may hold values from -0.21875 to 0.21875
- routes: int32 [16384, 8], P(('group', 'expert')), may hold values from 0 to 127, as said below
Outputs:
- hidden: bfloat16 [16384, 2048], P(('group', 'expert'))
- expert_mix: bfloat16 [16384, 2048], P(('group', 'expert'))
Inputs may be any that keep to these rules, and one draw needn't show every extreme that they name: `lengths`: one request has exactly 2048 valid tokens. `routes`: A row's 8 experts are different, and at most one of them is below 16. In the 64 rows of one device, each expert below 16 is named by at most 4 rows; in every such block some expert is named by exactly 4 rows, and one expert is named by exactly 4 rows in every block.
All inputs are finite; a program needn't handle non-finite values.
Results may differ from a plain program's by a relative error of at most 0.02.
Values may be sent and summed in bfloat16 or wider, within the bound.
A program may use at most 64 MiB of HBM per device.

v0:
```python
import math
import jax
import jax.numpy as jnp
from jax import lax
from jax.sharding import PartitionSpec as P

QUERY_HEADS = 32
KEY_VALUE_HEADS = 4
HEAD_DIMENSION = 128
epsilon = 1e-06
rope_theta = 1000000.0


def from_partner(block, axis, stride):
    count = lax.axis_size(axis)
    route = []
    for low in range(count):
        high = low | 1 << stride
        if high != low and high < count:
            route += [(low, high), (high, low)]
    return lax.ppermute(block, axis, route)


def norm_rows(values, gain_vector):
    widened = values.astype(jnp.float32)
    inverse_rms = lax.rsqrt(jnp.mean(widened * widened, axis=-1, keepdims=True) + epsilon)
    return widened * inverse_rms * gain_vector


def rotate(values, positions):
    half_width = values.shape[-1] // 2
    exponents = jnp.arange(half_width).astype(jnp.float32)
    inverse = jnp.exp(exponents * (-2.0 * math.log(rope_theta) / values.shape[-1]))
    angles = positions[:, None, None] * inverse[None, None, :]
    cosine_values = jnp.cos(angles)
    sine_values = jnp.sin(angles)
    first_half = values[..., :half_width]
    second = values[..., half_width:]
    return jnp.concatenate(
        [
            first_half * cosine_values - second * sine_values,
            second * cosine_values + first_half * sine_values,
        ],
        axis=-1,
    )


def local_positions(parity, row_count):
    indices = jnp.arange(row_count)
    quarter = row_count // 2
    offset = jnp.where(parity == 0, jnp.where(indices < quarter, 0, 2 * quarter), quarter)
    return indices + offset


def per_device(
    hidden_in,
    norm_attention,
    norm_experts,
    query_master,
    trainer_key_value_weight,
    output_master,
    query_gain,
    key_gain,
    lengths,
    router,
    expert_gateup,
    expert_down,
    routes,
):
    experts_axis = lax.axis_size("expert")
    group_member = lax.axis_index("expert")
    group_index = lax.axis_index("group")
    local_head_count = QUERY_HEADS // experts_axis
    width_here = local_head_count * HEAD_DIMENSION
    common_head = group_member * local_head_count // (QUERY_HEADS // KEY_VALUE_HEADS)
    keyvalue_slice = lax.dynamic_slice_in_dim(
        trainer_key_value_weight, common_head * HEAD_DIMENSION, HEAD_DIMENSION, 2
    ).astype(jnp.bfloat16)
    query_full, keyvalue_full, output_part = (
        lax.all_gather(query_master.astype(jnp.bfloat16), "group", axis=0, tiled=True),
        lax.all_gather(keyvalue_slice, "group", axis=1, tiled=True),
        lax.all_gather(output_master.astype(jnp.bfloat16), "group", axis=1, tiled=True),
    )
    joined_weights = jnp.concatenate([query_full, keyvalue_full[0], keyvalue_full[1]], axis=1)
    normed = norm_rows(hidden_in, norm_attention).astype(jnp.bfloat16)
    projected = jnp.dot(
        lax.all_gather(normed, "expert", axis=0, tiled=True),
        joined_weights,
        preferred_element_type=jnp.float32,
    ).astype(jnp.bfloat16)
    local_rows = projected.shape[0]
    query_rows_list = projected[:, :width_here].reshape(
        local_rows, local_head_count, HEAD_DIMENSION
    )
    key_rows = projected[:, width_here : width_here + HEAD_DIMENSION]
    value_rows = projected[:, width_here + HEAD_DIMENSION :]
    parity = group_index % 2
    own_places = local_positions(parity, local_rows)
    partner_places = local_positions(1 - parity, local_rows)
    query_rows_list = rotate(
        norm_rows(query_rows_list, query_gain), own_places.astype(jnp.float32)
    ).astype(jnp.bfloat16)
    key_rows = rotate(norm_rows(key_rows[:, None, :], key_gain), own_places.astype(jnp.float32))[
        :, 0, :
    ].astype(jnp.bfloat16)
    partner = from_partner(jnp.stack([key_rows, value_rows]), "group", 0)
    all_keys = jnp.concatenate([key_rows, partner[0]], axis=0)
    all_values = jnp.concatenate([value_rows, partner[1]], axis=0)
    key_places = jnp.concatenate([own_places, partner_places])
    valid_length = jnp.sum(jnp.where(jnp.arange(lengths.shape[0]) == group_index // 2, lengths, 0))
    block_rows = min(512, local_rows)
    block_count = local_rows // block_rows
    score_scale = HEAD_DIMENSION ** (-0.5)

    def attend(block_index):
        block_start = block_index * block_rows
        query_block = lax.dynamic_slice_in_dim(query_rows_list, block_start, block_rows, 0)
        query_places = lax.dynamic_slice_in_dim(own_places, block_start, block_rows, 0)
        scores = (
            jnp.einsum("qhd,kd->hqk", query_block, all_keys, preferred_element_type=jnp.float32)
            * score_scale
        )
        allowed = (key_places[None, :] <= query_places[:, None]) & (
            key_places[None, :] < valid_length
        )
        weights = jnp.where(allowed[None], jnp.exp(scores), 0.0)
        denominators = jnp.sum(weights, axis=-1)
        weighted = jnp.einsum(
            "hqk,kd->qhd",
            weights.astype(jnp.bfloat16),
            all_values,
            preferred_element_type=jnp.float32,
        )
        return (weighted / jnp.transpose(denominators)[:, :, None]).astype(jnp.bfloat16)

    attended = lax.map(attend, jnp.arange(block_count)).reshape(local_rows, width_here)
    summed = lax.psum_scatter(
        jnp.dot(attended, output_part, preferred_element_type=jnp.float32).astype(jnp.bfloat16),
        "expert",
        scatter_dimension=0,
        tiled=True,
    ).astype(jnp.float32)
    hidden = (hidden_in.astype(jnp.float32) + summed).astype(jnp.bfloat16)
    normed_second = norm_rows(hidden, norm_experts).astype(jnp.bfloat16)
    logits = jnp.dot(normed_second, router, preferred_element_type=jnp.float32)
    route_table = routes[:, :, None] == jnp.arange(logits.shape[1])[None, None, :]
    picked = jnp.sum(jnp.where(route_table, logits[:, None, :], 0.0), axis=-1)
    raised = jnp.exp(picked)
    gate_values = raised / jnp.sum(raised, axis=1, keepdims=True)
    inside = routes < experts_axis
    gate_window = jnp.sum(jnp.where(inside, gate_values, 0.0), axis=1)
    expert_window = jnp.sum(jnp.where(inside, routes, 0), axis=1)
    present = jnp.any(inside, axis=1)
    capacity = local_rows // (experts_axis * experts_axis)
    member_table = (
        present[:, None] & (expert_window[:, None] == jnp.arange(experts_axis)[None, :])
    ).astype(jnp.int32)
    ranking = jnp.sum(jnp.cumsum(member_table, axis=0) * member_table, axis=1) - 1
    slot_index = expert_window * capacity + ranking
    select = (
        (jnp.arange(experts_axis * capacity)[:, None] == slot_index[None, :]) & present[None, :]
    ).astype(jnp.bfloat16)
    model_width = normed_second.shape[1]
    outgoing = (
        jnp.dot(select, normed_second, preferred_element_type=jnp.float32)
        .astype(jnp.bfloat16)
        .reshape(experts_axis, capacity, model_width)
    )
    gateup_here = expert_gateup[0]
    down_here = expert_down[0]
    hidden_units = down_here.shape[0]
    slot_items = lax.all_to_all(outgoing, "expert", split_axis=0, concat_axis=0, tiled=True)
    flattened = slot_items.reshape(-1, slot_items.shape[-1])
    gate_up = jnp.dot(flattened, gateup_here, preferred_element_type=jnp.float32)
    active = (jax.nn.silu(gate_up[:, :hidden_units]) * gate_up[:, hidden_units:]).astype(
        jnp.bfloat16
    )
    result = (
        jnp.dot(active, down_here, preferred_element_type=jnp.float32)
        .astype(jnp.bfloat16)
        .reshape(slot_items.shape)
    )
    returned = lax.all_to_all(result, "expert", split_axis=0, concat_axis=0, tiled=True)
    combined = jnp.dot(
        jnp.transpose(select), returned.reshape(-1, model_width), preferred_element_type=jnp.float32
    )
    expert_mix = (gate_window[:, None] * combined).astype(jnp.bfloat16)
    return (hidden, expert_mix)


def solution(mesh):
    return jax.shard_map(
        per_device,
        mesh=mesh,
        in_specs=(
            P(("group", "expert"), None),
            P(),
            P(),
            P("group", "expert"),
            P(None, "group", None),
            P("expert", "group"),
            P(),
            P(),
            P(),
            P(),
            P("expert", None, None),
            P("expert", None, None),
            P(("group", "expert"), None),
        ),
        out_specs=(P(("group", "expert"), None), P(("group", "expert"), None)),
        check_vma=False,
    )
```

profile of v0, /device:TPU:1, one launch (start us, length us, event | category | flops | bytes accessed | tf_op | source)
XLA Modules:
  0.0 400.9 jit_solution(13658261090532443639)
XLA Ops:
  7.2 1.7 dynamic-slice_convert_fusion
  9.0 1.5 convert_element_type.103
  10.6 1.1 fusion.36
  11.7 1.8 fusion.38
  13.6 1.5 convert_element_type.114
  15.3 3.1 multiply_cosine_fusion
  18.4 1.4 fusion.68
  19.7 69.8 %all-gather.9.cloned.1.call-done = bf16[2,2048,128]{2,1,0:T(8,128)(2,1)} async-done(((bf16[2,128,128]{2,1,0:T(8,128)(2,1)}), bf16[2,2048,128]{2,1,0:T(8,128)(2,1)}) %all-gather.9.cloned.1.call-update) | async-done | bytes 1048592 | tf_op jit(solution)/shard_map/all_gather | solution.py:81
  89.6 2.3 slice_bitcast_fusion.1
  91.9 75.7 %all-gather.7.cloned.1.call-done = bf16[2048,256]{1,0:T(8,128)(2,1)} async-done(((bf16[128,256]{1,0:T(8,128)(2,1)}), bf16[2048,256]{1,0:T(8,128)(2,1)}) %all-gather.7.cloned.1.call-update) | async-done | bytes 1048592 | tf_op jit(solution)/shard_map/all_gather | solution.py:80
  167.6 43.1 %all-gather.5.cloned.1.call-done = bf16[1024,2048]{1,0:T(8,128)(2,1)} async-done(((bf16[64,2048]{1,0:T(8,128)(2,1)}), bf16[1024,2048]{1,0:T(8,128)(2,1)}) %all-gather.5.cloned.1.call-update) | async-done | bytes 4194320 | tf_op jit(solution)/shard_map/all_gather | solution.py:87
  210.7 5.2 %fusion.27 = bf16[1024,512]{0,1:T(8,128)(2,1)S(1)} fusion(bf16[1024,2048]{1,0:T(8,128)(2,1)} %all-gather.5.cloned.1.call-done, bf16[2048,128]{1,0:T(8,128)(2,1)} %get-tuple-element.104, bf16[2048,128]{1,0:T(8,128)(2,1)} %get-tuple-element.103, bf16[2048,256]{1,0:T(8,128)(2,1)} %all-gather.7.cloned.1.call-done), kind=kOutput, calls=%fused_computation.34 | convolution fusion | flops 2154299392 | bytes 7340032 | tf_op jit(solution)/shard_map/dot_general | solution.py:86
  216.0 0.8 slice.54
  217.1 1.2 fusion.46
  219.0 0.9 pad_maximum_fusion.1
  219.8 2.4 collective-permute-start
  222.3 2.2 copy.24
  224.5 1.6 multiply_multiply_fusion
  226.1 1.7 subtract_convert_fusion
  227.8 1.1 pad_maximum_fusion
  228.9 6.7 %collective-permute-done = bf16[2,1024,128]{1,2,0:T(8,128)(2,1)} collective-permute-done((bf16[2,1024,128]{1,2,0:T(8,128)(2,1)}, bf16[2,1024,128]{1,2,0:T(8,128)(2,1)}, u32[]{:S(2)}, u32[]{:S(2)}) %collective-permute-start) | collective-permute-done | bytes 524320 | tf_op jit(solution)/shard_map/ppermute | solution.py:21
  235.6 1.1 slice_bitcast_fusion.2
  236.7 1.1 pad_maximum_fusion.2
  237.8 2.1 copy.25
  239.8 2.1 copy.26
  241.9 19.4 %while.10 = (s32[]{:T(128)}, bf16[2,512,2,128]{3,2,1,0:T(2,128)(2,1)}, s32[2048]{0:T(1024)S(1)}, s32[2]{0:T(128)S(1)}, s32[1024]{0:T(1024)S(1)}, /*index=5*/s32[...) while((s32[]{:T(128)}, ...), condition=%wide.region_6.7_spmd, body=%wide.region_4.6_spmd.sunk | while | flops 1088685056 | bytes 24152800 | solution.py:136
  243.9 0.7 compare_and_fusion.2
  244.6 3.9 bitcast_reduce_fusion.2
  248.5 2.0 fusion.82
  250.6 1.0 copy_dynamic-update-slice_fusion.2
  254.3 3.9 bitcast_reduce_fusion.2
  258.2 2.0 fusion.82
  260.3 1.0 copy_dynamic-update-slice_fusion.2
  261.3 24.7 %all-gather.11.cloned.1.call-done = bf16[256,2048]{1,0:T(8,128)(2,1)} async-done(((bf16[256,128]{1,0:T(8,128)(2,1)}), bf16[256,2048]{1,0:T(8,128)(2,1)}) %all-gather.11.cloned.1.call-update) | async-done | bytes 1048592 | tf_op jit(solution)/shard_map/all_gather | solution.py:82
  286.0 4.6 %convolution_convert_fusion = bf16[1024,2048]{1,0:T(8,128)(2,1)} fusion(bf16[256,2048]{1,0:T(8,128)(2,1)} %all-gather.11.cloned.1.call-done, bf16[128,8,2,128]{3,2,1,0:T(2,128)(2,1)} %bitcast.20), kind=kOutput, calls=%fused_computation.21 | convolution fusion | flops 1075838976 | bytes 5767168 | tf_op jit(solution)/shard_map/dot_general | solution.py:138
  291.3 64.7 %reduce-scatter.2.cloned.1.call-done = bf16[64,2048]{1,0:T(8,128)(2,1)} async-done(((bf16[1024,2048]{1,0:T(8,128)(2,1)}), bf16[64,2048]{1,0:T(8,128)(2,1)}) %reduce-scatter.2.cloned.1.call-update) | async-done | bytes 262160 | tf_op jit(solution)/shard_map/reduce_scatter | solution.py:137
  356.0 1.1 fusion.33
  358.2 0.8 reshape.264
  359.0 7.5 %all-to-all-start = ((bf16[16,4,2048]{2,1,0:T(4,128)(2,1)}), bf16[16,4,2048]{2,1,0:T(4,128)(2,1)S(1)}, u32[]{:S(2)}, u32[]{:S(2)}) async-start(bf16[16,4,2048]{2,1,0:T(4,128)(2,1)} %reshape.264), calls=%async_computation.1 | async-start | bytes 524288 | tf_op jit(solution)/shard_map/all_to_all | solution.py:172
  366.5 1.4 fusion.52
  367.9 5.8 %all-to-all-done = bf16[16,4,2048]{2,1,0:T(4,128)(2,1)S(1)} async-done(((bf16[16,4,2048]{2,1,0:T(4,128)(2,1)}), bf16[16,4,2048]{2,1,0:T(4,128)(2,1)S(1)}, u32[]{:S(2)}, u32[]{:S(2)}) %all-to-all-start) | async-done | bytes 262176 | tf_op jit(solution)/shard_map/all_to_all | solution.py:172
  373.8 0.8 reshape.265
  374.5 4.0 %fusion.13 = f32[64,1536]{1,0:T(8,128)S(1)} fusion(bf16[64,2048]{1,0:T(8,128)(2,1)} %reshape.265, bf16[1,2048,1536]{2,1,0:T(8,128)(2,1)} %param.25), kind=kOutput, calls=%fused_computation.19 | convolution fusion | flops 402653184 | bytes 6946816 | tf_op jit(solution)/shard_map/dot_general | solution.py:174
  379.3 0.8 reshape.266
  380.1 4.9 %all-to-all-start.1 = ((bf16[16,4,2048]{2,1,0:T(4,128)(2,1)}), bf16[16,4,2048]{2,1,0:T(4,128)(2,1)}, u32[]{:S(2)}, u32[]{:S(2)}) async-start(bf16[16,4,2048]{2,1,0:T(4,128)(2,1)} %reshape.266), calls=%async_computation.2 | async-start | bytes 524288 | tf_op jit(solution)/shard_map/all_to_all | solution.py:183
  385.5 6.8 %all-to-all-done.1 = bf16[16,4,2048]{2,1,0:T(4,128)(2,1)} async-done(((bf16[16,4,2048]{2,1,0:T(4,128)(2,1)}), bf16[16,4,2048]{2,1,0:T(4,128)(2,1)}, u32[]{:S(2)}, u32[]{:S(2)}) %all-to-all-start.1) | async-done | bytes 262176 | tf_op jit(solution)/shard_map/all_to_all | solution.py:183
  392.3 1.0 reshape.267
  393.4 1.0 fusion.17
  (64 shorter events, 7.7 us)
Async XLA Ops:
  7.2 371.4 %copy-start = (bf16[1,768,2048]{2,1,0:T(8,128)(2,1)S(1)}, bf16[1,768,2048]{2,1,0:T(8,128)(2,1)}, u32[]{:S(2)}) copy-start(bf16[1,768,2048]{2,1,0:T(8,128)(2,1)} %param.26) | copy-start | bytes 9437188
  7.2 82.4 %all-gather.9.cloned.1.call-start = ((), (), s32[]{:S(2)}) async-start(), calls=%async_computation.5 | async-start | bytes 1114112 | tf_op jit(solution)/shard_map/all_gather | solution.py:81
  9.0 158.6 %all-gather.7.cloned.1.call-start = ((), (), s32[]{:S(2)}) async-start(), calls=%async_computation.4 | async-start | bytes 1114112 | tf_op jit(solution)/shard_map/all_gather | solution.py:80
  10.6 200.1 %all-gather.5.cloned.1.call-start = ((), (), s32[]{:S(2)}) async-start(), calls=%async_computation.3 | async-start | bytes 4456448 | tf_op jit(solution)/shard_map/all_gather | solution.py:87
  13.5 272.4 %all-gather.11.cloned.1.call-start = ((), (), s32[]{:S(2)}) async-start(), calls=%async_computation.6 | async-start | bytes 1114112 | tf_op jit(solution)/shard_map/all_gather | solution.py:82
  15.2 340.9 %reduce-scatter.2.cloned.1.call-start = ((), (), s32[]{:S(2)}) async-start(), calls=%async_computation.7 | async-start | bytes 4456448 | tf_op jit(solution)/shard_map/reduce_scatter | solution.py:137
  210.6 6.3 %copy-start.8 = (f32[128]{0:T(128)S(1)}, f32[128]{0:T(128)}, u32[]{:S(2)}) copy-start(f32[128]{0:T(128)} %param.22) | copy-start | bytes 1540
  215.8 8.7 %copy-start.7 = (f32[128]{0:T(128)S(1)}, f32[128]{0:T(128)}, u32[]{:S(2)}) copy-start(f32[128]{0:T(128)} %param.21) | copy-start | bytes 1540
  219.8 15.8 %collective-permute-start = (bf16[2,1024,128]{1,2,0:T(8,128)(2,1)}, bf16[2,1024,128]{1,2,0:T(8,128)(2,1)}, u32[]{:S(2)}, u32[]{:S(2)}) collective-permute-start(bf16[2,1024,128]{1,2,0:T(8,128)(2,1)} %pad_maximum_fusion.1), channel_id=1, source_target_pairs={{0,16},{16,0},{32,48},{48,32},{64,80},{80,64},{96,112},{112,96},{1... | collective-permute-start | bytes 1572872 | tf_op jit(solution)/shard_map/ppermute | solution.py:21
  224.5 12.2 %copy-start.3 = (bf16[1024,128]{0,1:T(8,128)(2,1)S(1)}, bf16[1024,128]{0,1:T(8,128)(2,1)}, u32[]{:S(2)}) copy-start(bf16[1024,128]{0,1:T(8,128)(2,1)} %get-tuple-element.109) | copy-start | bytes 786436
  244.6 3.9 copy-start.4
  254.3 3.9 copy-start.4
  286.0 4.6 %copy-start.6 = (s32[64,8]{0,1:T(8,128)S(1)}, s32[64,8]{0,1:T(8,128)}, u32[]{:S(2)}) copy-start(s32[64,8]{0,1:T(8,128)} %param.27) | copy-start | bytes 6148
  290.6 65.5 %copy-start.1 = (bf16[64,2048]{1,0:T(8,128)(2,1)S(1)}, bf16[64,2048]{1,0:T(8,128)(2,1)}, u32[]{:S(2)}) copy-start(bf16[64,2048]{1,0:T(8,128)(2,1)} %param.15) | copy-start | bytes 786436
  290.6 67.3 %copy-start.5 = (f32[2048]{0:T(1024)S(1)}, f32[2048]{0:T(1024)}, u32[]{:S(2)}) copy-start(f32[2048]{0:T(1024)} %param.17) | copy-start | bytes 24580
  357.2 0.7 copy-start.2
  359.0 14.8 %all-to-all-start = ((bf16[16,4,2048]{2,1,0:T(4,128)(2,1)}), bf16[16,4,2048]{2,1,0:T(4,128)(2,1)S(1)}, u32[]{:S(2)}, u32[]{:S(2)}) async-start(bf16[16,4,2048]{2,1,0:T(4,128)(2,1)} %reshape.264), calls=%async_computation.1 | async-start | bytes 524288 | tf_op jit(solution)/shard_map/all_to_all | solution.py:172
  380.1 12.3 %all-to-all-start.1 = ((bf16[16,4,2048]{2,1,0:T(4,128)(2,1)}), bf16[16,4,2048]{2,1,0:T(4,128)(2,1)}, u32[]{:S(2)}, u32[]{:S(2)}) async-start(bf16[16,4,2048]{2,1,0:T(4,128)(2,1)} %reshape.266), calls=%async_computation.2 | async-start | bytes 524288 | tf_op jit(solution)/shard_map/all_to_all | solution.py:183
Sparse Core Ops, SparseCore 0:
  10.6 78.9 all-gather.8
  92.1 75.3 all-gather.6
  170.0 40.6 all-gather.4
  213.5 72.3 all-gather.10
  290.7 65.2 reduce-scatter.1
where the time goes:
time: 402 us; the launch traced here: 401 us
  waiting for transfers between devices  297 us (74%)
  matrix products  29 us (7%)
  other arithmetic  24.1 us (6%)
  local copies, waits for them, and re-layouts  19.8 us (5%)
  starting transfers between devices  15.1 us (4%)
  between operations  14.1 us (4%)
    all_gather x1, waiting for transfers between devices, per_device(): lax.all_gather(query_master.astype(jnp.bfloat16), 'group', axis=0, tiled=...  75.7 us
    all_gather x1, waiting for transfers between devices, per_device(): lax.all_gather(keyvalue_slice, 'group', axis=1, tiled=True)  69.8 us
    reduce_scatter x1, waiting for transfers between devices, per_device(): lax.psum_scatter(jnp.dot(attended, output_part, preferred_element_type=jn...  64.7 us
    all_gather x1, waiting for transfers between devices, per_device(): lax.all_gather(normed, 'expert', axis=0, tiled=True)  43.1 us
    all_gather x1, waiting for transfers between devices, per_device(): lax.all_gather(output_master.astype(jnp.bfloat16), 'group', axis=1, tiled...  24.7 us
  transfers between devices with their start and end apart: 8, of which 8 were waited for; matrix products, arithmetic and copies ran while one was open for 14% of the time, Pallas kernels for 0%

commit v1 on v0

--- a/solution.py
+++ b/solution.py
@@ -77,7 +77,15 @@
         trainer_key_value_weight, common_head * HEAD_DIMENSION, HEAD_DIMENSION, 2
     ).astype(jnp.bfloat16)
     query_full, keyvalue_full, output_part = (
-        lax.all_gather(query_master.astype(jnp.bfloat16), "group", axis=0, tiled=True),
+        jnp.concatenate(
+            lax.all_to_all(
+                jnp.stack([query_master.astype(jnp.bfloat16)] * lax.axis_size("group")),
+                "group",
+                0,
+                0,
+            ),
+            axis=0,
+        ),
         lax.all_gather(keyvalue_slice, "group", axis=1, tiled=True),
         lax.all_gather(output_master.astype(jnp.bfloat16), "group", axis=1, tiled=True),
     )

time: 402 us -> 330 us (0.82)
  waiting for transfers between devices: 297 us -> 215 us
  starting transfers between devices: 15.1 us -> 26.6 us
    all_gather x1 -> x0, waiting for transfers between devices: 75.7 us -> none  [per_device(): lax.all_gather(query_master.astype(jnp.bfloat16), 'group', axis=0, tiled=...]
    all_to_all x0 -> x1, starting transfers between devices: none -> 11.6 us  [per_device(): lax.all_to_all(jnp.stack([query_master.astype(jnp.bfloat16)] * lax.axis_s...]
    all_gather x1, waiting for transfers between devices: 69.8 us -> 65.1 us  [per_device(): lax.all_gather(keyvalue_slice, 'group', axis=1, tiled=True)]
  transfers between devices with their start and end apart: 8 -> 8, of which waited for: 8 -> 7; matrix products, arithmetic and copies ran while one was open for 14% -> 16% of each run, Pallas kernels for 0% -> 0%
where the time goes in v1:
time: 330 us; the launch traced here: 329 us
  waiting for transfers between devices  215 us (65%)
  matrix products  29 us (9%)
  starting transfers between devices  26.6 us (8%)
  other arithmetic  21.7 us (7%)
  local copies, waits for them, and re-layouts  20.9 us (6%)
  between operations  14.1 us (4%)
    all_gather x1, waiting for transfers between devices, per_device(): lax.all_gather(keyvalue_slice, 'group', axis=1, tiled=True)  65.1 us
    reduce_scatter x1, waiting for transfers between devices, per_device(): lax.psum_scatter(jnp.dot(attended, output_part, preferred_element_type=jn...  64.9 us
    all_gather x1, waiting for transfers between devices, per_device(): lax.all_gather(normed, 'expert', axis=0, tiled=True)  40.8 us
    all_gather x1, waiting for transfers between devices, per_device(): lax.all_gather(output_master.astype(jnp.bfloat16), 'group', axis=1, tiled...  25 us
    all_to_all x1, starting transfers between devices, per_device(): lax.all_to_all(jnp.stack([query_master.astype(jnp.bfloat16)] * lax.axis_s...  11.6 us
    dot_general x2, matrix products, attend(): jnp.einsum('qhd,kd->hqk', query_block, all_keys, preferred_element_type=j...  7.79 us
    all_to_all x1, starting transfers between devices, per_device(): lax.all_to_all(outgoing, 'expert', split_axis=0, concat_axis=0, tiled=True)  7.51 us
    all_to_all x1, waiting for transfers between devices, per_device(): lax.all_to_all(result, 'expert', split_axis=0, concat_axis=0, tiled=True)  6.81 us
  transfers between devices with their start and end apart: 8, of which 7 were waited for; matrix products, arithmetic and copies ran while one was open for 16% of the time, Pallas kernels for 0%

profile of v1, /device:TPU:1, one launch (start us, length us, event | category | flops | bytes accessed | tf_op | source)
XLA Modules:
  0.0 328.9 jit_solution(655260516945171667)
XLA Ops:
  7.3 1.7 dynamic-slice_convert_fusion
  9.0 1.1 fusion.36
  10.1 1.8 fusion.38
  12.0 0.9 convert_element_type.103
  12.9 1.1 stack.6
  14.0 11.6 %all-to-all-start = ((bf16[16,128,256]{2,1,0:T(8,128)(2,1)}), bf16[16,128,256]{2,1,0:T(8,128)(2,1)}, u32[]{:S(2)}, u32[]{:S(2)}) async-start(bf16[16,128,256]{2,1,0:T(8,128)(2,1)} %stack.6), calls=%async_computation | async-start | bytes 2097152 | tf_op jit(solution)/shard_map/all_to_all | solution.py:81
  27.1 3.1 multiply_cosine_fusion
  30.2 65.1 %all-gather.6.cloned.1.call-done = bf16[2,2048,128]{2,1,0:T(8,128)(2,1)} async-done(((bf16[2,128,128]{2,1,0:T(8,128)(2,1)}), bf16[2,2048,128]{2,1,0:T(8,128)(2,1)}) %all-gather.6.cloned.1.call-update) | async-done | bytes 1048592 | tf_op jit(solution)/shard_map/all_gather | solution.py:89
  95.3 2.3 slice_bitcast_fusion.1
  97.6 40.8 %all-gather.4.cloned.1.call-done = bf16[1024,2048]{1,0:T(8,128)(2,1)} async-done(((bf16[64,2048]{1,0:T(8,128)(2,1)}), bf16[1024,2048]{1,0:T(8,128)(2,1)}) %all-gather.4.cloned.1.call-update) | async-done | bytes 4194320 | tf_op jit(solution)/shard_map/all_gather | solution.py:95
  138.4 5.2 %fusion.27 = bf16[1024,512]{0,1:T(8,128)(2,1)S(1)} fusion(bf16[1024,2048]{1,0:T(8,128)(2,1)} %all-gather.4.cloned.1.call-done, bf16[2048,128]{1,0:T(8,128)(2,1)} %get-tuple-element.104, bf16[2048,128]{1,0:T(8,128)(2,1)} %get-tuple-element.103, bf16[2048,256]{1,0:T(8,128)(2,1)} %bitcast.7), kind=kOutput, calls=%fused_computation.34 | convolution fusion | flops 2154299392 | bytes 7340032 | tf_op jit(solution)/shard_map/dot_general | solution.py:94
  143.7 0.8 slice.54
  144.8 1.2 fusion.46
  146.7 0.9 pad_maximum_fusion.1
  147.5 2.4 collective-permute-start
  150.0 2.2 copy.24
  152.2 1.6 multiply_multiply_fusion
  153.8 1.7 subtract_convert_fusion
  155.5 1.1 pad_maximum_fusion
  156.6 6.7 %collective-permute-done = bf16[2,1024,128]{1,2,0:T(8,128)(2,1)} collective-permute-done((bf16[2,1024,128]{1,2,0:T(8,128)(2,1)}, bf16[2,1024,128]{1,2,0:T(8,128)(2,1)}, u32[]{:S(2)}, u32[]{:S(2)}) %collective-permute-start) | collective-permute-done | bytes 524320 | tf_op jit(solution)/shard_map/ppermute | solution.py:21
  163.3 1.1 slice_bitcast_fusion.2
  164.4 1.1 pad_maximum_fusion.2
  165.5 2.1 copy.25
  167.5 2.0 copy.26
  169.6 19.3 %while.10 = (s32[]{:T(128)}, bf16[2,512,2,128]{3,2,1,0:T(2,128)(2,1)}, s32[2048]{0:T(1024)S(1)}, s32[2]{0:T(128)S(1)}, s32[1024]{0:T(1024)S(1)}, /*index=5*/s32[...) while((s32[]{:T(128)}, ...), condition=%wide.region_6.7_spmd, body=%wide.region_4.6_spmd.sunk | while | flops 1088685056 | bytes 24152800 | solution.py:144
  171.5 0.7 compare_and_fusion.2
  172.3 3.9 %bitcast_reduce_fusion.2 = (f32[2,512]{1,0:T(2,128)S(1)}, f32[512,2,2048]{2,0,1:T(8,128)S(1)}) fusion(pred[512,2048]{1,0:T(8,128)(4,1)S(1)} %compare_and_fusion.2, bf16[2048,128]{1,0:T(8,128)(2,1)} %get-tuple-element.209, bf16[1024,2,128]{2,0,1:T(8,128)(2,1)} %get-tuple-element.208, s32[]{:T(128)S(6)} %select_n.131), kind=kOutput, calls=%fused_computation.clone.1 | convolution fusion | flops 543161344 | bytes 10227716 | tf_op jit(solution)/shard_map/while/body/eval_jaxpr/qhd,kd->hqk/dot_general | solution.py:128
  176.2 2.0 fusion.82
  178.2 1.0 copy_dynamic-update-slice_fusion.2
  181.2 0.7 compare_and_fusion.2
  182.0 3.9 %bitcast_reduce_fusion.2 = (f32[2,512]{1,0:T(2,128)S(1)}, f32[512,2,2048]{2,0,1:T(8,128)S(1)}) fusion(pred[512,2048]{1,0:T(8,128)(4,1)S(1)} %compare_and_fusion.2, bf16[2048,128]{1,0:T(8,128)(2,1)} %get-tuple-element.209, bf16[1024,2,128]{2,0,1:T(8,128)(2,1)} %get-tuple-element.208, s32[]{:T(128)S(6)} %select_n.131), kind=kOutput, calls=%fused_computation.clone.1 | convolution fusion | flops 543161344 | bytes 10227716 | tf_op jit(solution)/shard_map/while/body/eval_jaxpr/qhd,kd->hqk/dot_general | solution.py:128
  185.9 2.0 fusion.82
  187.9 1.0 copy_dynamic-update-slice_fusion.2
  188.9 25.0 %all-gather.8.cloned.1.call-done = bf16[256,2048]{1,0:T(8,128)(2,1)} async-done(((bf16[256,128]{1,0:T(8,128)(2,1)}), bf16[256,2048]{1,0:T(8,128)(2,1)}) %all-gather.8.cloned.1.call-update) | async-done | bytes 1048592 | tf_op jit(solution)/shard_map/all_gather | solution.py:90
  213.9 4.6 %convolution_convert_fusion = bf16[1024,2048]{1,0:T(8,128)(2,1)} fusion(bf16[256,2048]{1,0:T(8,128)(2,1)} %all-gather.8.cloned.1.call-done, bf16[128,8,2,128]{3,2,1,0:T(2,128)(2,1)} %bitcast.21), kind=kOutput, calls=%fused_computation.21 | convolution fusion | flops 1075838976 | bytes 5767168 | tf_op jit(solution)/shard_map/dot_general | solution.py:146
  219.2 64.9 %reduce-scatter.2.cloned.1.call-done = bf16[64,2048]{1,0:T(8,128)(2,1)} async-done(((bf16[1024,2048]{1,0:T(8,128)(2,1)}), bf16[64,2048]{1,0:T(8,128)(2,1)}) %reduce-scatter.2.cloned.1.call-update) | async-done | bytes 262160 | tf_op jit(solution)/shard_map/reduce_scatter | solution.py:145
  284.1 1.1 fusion.33
  286.3 0.8 reshape.270
  287.1 7.5 %all-to-all-start.1 = ((bf16[16,4,2048]{2,1,0:T(4,128)(2,1)}), bf16[16,4,2048]{2,1,0:T(4,128)(2,1)S(1)}, u32[]{:S(2)}, u32[]{:S(2)}) async-start(bf16[16,4,2048]{2,1,0:T(4,128)(2,1)} %reshape.270), calls=%async_computation.2 | async-start | bytes 524288 | tf_op jit(solution)/shard_map/all_to_all | solution.py:180
  294.6 1.4 fusion.52
  296.0 5.8 %all-to-all-done.1 = bf16[16,4,2048]{2,1,0:T(4,128)(2,1)S(1)} async-done(((bf16[16,4,2048]{2,1,0:T(4,128)(2,1)}), bf16[16,4,2048]{2,1,0:T(4,128)(2,1)S(1)}, u32[]{:S(2)}, u32[]{:S(2)}) %all-to-all-start.1) | async-done | bytes 262176 | tf_op jit(solution)/shard_map/all_to_all | solution.py:180
  301.8 0.8 reshape.271
  302.6 4.0 %fusion.13 = f32[64,1536]{1,0:T(8,128)S(1)} fusion(bf16[64,2048]{1,0:T(8,128)(2,1)} %reshape.271, bf16[1,2048,1536]{2,1,0:T(8,128)(2,1)} %param.25), kind=kOutput, calls=%fused_computation.19 | convolution fusion | flops 402653184 | bytes 6946816 | tf_op jit(solution)/shard_map/dot_general | solution.py:182
  307.3 0.8 reshape.272
  308.1 4.9 %all-to-all-start.2 = ((bf16[16,4,2048]{2,1,0:T(4,128)(2,1)}), bf16[16,4,2048]{2,1,0:T(4,128)(2,1)}, u32[]{:S(2)}, u32[]{:S(2)}) async-start(bf16[16,4,2048]{2,1,0:T(4,128)(2,1)} %reshape.272), calls=%async_computation.3 | async-start | bytes 524288 | tf_op jit(solution)/shard_map/all_to_all | solution.py:191
  313.6 6.8 %all-to-all-done.2 = bf16[16,4,2048]{2,1,0:T(4,128)(2,1)} async-done(((bf16[16,4,2048]{2,1,0:T(4,128)(2,1)}), bf16[16,4,2048]{2,1,0:T(4,128)(2,1)}, u32[]{:S(2)}, u32[]{:S(2)}) %all-to-all-start.2) | async-done | bytes 262176 | tf_op jit(solution)/shard_map/all_to_all | solution.py:191
  320.4 1.0 reshape.273
  321.4 1.0 fusion.17
  (68 shorter events, 8.1 us)
Async XLA Ops:
  7.2 299.5 %copy-start = (bf16[1,768,2048]{2,1,0:T(8,128)(2,1)S(1)}, bf16[1,768,2048]{2,1,0:T(8,128)(2,1)}, u32[]{:S(2)}) copy-start(bf16[1,768,2048]{2,1,0:T(8,128)(2,1)} %param.26) | copy-start | bytes 9437188
  7.2 18.5 %copy-start.5 = (f32[256,128]{1,0:T(8,128)S(1)}, f32[256,128]{1,0:T(8,128)}, u32[]{:S(2)}) copy-start(f32[256,128]{1,0:T(8,128)} %param.20) | copy-start | bytes 393220
  7.2 19.3 %copy-start.10 = (s32[8]{0:T(128)S(1)}, s32[8]{0:T(128)}, u32[]{:S(2)}) copy-start(s32[8]{0:T(128)} %param.23) | copy-start | bytes 100
  7.2 88.1 %all-gather.6.cloned.1.call-start = ((), (), s32[]{:S(2)}) async-start(), calls=%async_computation.5 | async-start | bytes 1114112 | tf_op jit(solution)/shard_map/all_gather | solution.py:89
  9.0 129.4 %all-gather.4.cloned.1.call-start = ((), (), s32[]{:S(2)}) async-start(), calls=%async_computation.4 | async-start | bytes 4456448 | tf_op jit(solution)/shard_map/all_gather | solution.py:95
  14.0 83.6 %all-to-all-start = ((bf16[16,128,256]{2,1,0:T(8,128)(2,1)}), bf16[16,128,256]{2,1,0:T(8,128)(2,1)}, u32[]{:S(2)}, u32[]{:S(2)}) async-start(bf16[16,128,256]{2,1,0:T(8,128)(2,1)} %stack.6), calls=%async_computation | async-start | bytes 2097152 | tf_op jit(solution)/shard_map/all_to_all | solution.py:81
  25.6 188.3 %all-gather.8.cloned.1.call-start = ((), (), s32[]{:S(2)}) async-start(), calls=%async_computation.6 | async-start | bytes 1114112 | tf_op jit(solution)/shard_map/all_gather | solution.py:90
  26.3 257.8 %reduce-scatter.2.cloned.1.call-start = ((), (), s32[]{:S(2)}) async-start(), calls=%async_computation.7 | async-start | bytes 4456448 | tf_op jit(solution)/shard_map/reduce_scatter | solution.py:145
  138.4 6.3 %copy-start.9 = (f32[128]{0:T(128)S(1)}, f32[128]{0:T(128)}, u32[]{:S(2)}) copy-start(f32[128]{0:T(128)} %param.22) | copy-start | bytes 1540
  143.6 8.6 %copy-start.8 = (f32[128]{0:T(128)S(1)}, f32[128]{0:T(128)}, u32[]{:S(2)}) copy-start(f32[128]{0:T(128)} %param.21) | copy-start | bytes 1540
  147.5 15.8 %collective-permute-start = (bf16[2,1024,128]{1,2,0:T(8,128)(2,1)}, bf16[2,1024,128]{1,2,0:T(8,128)(2,1)}, u32[]{:S(2)}, u32[]{:S(2)}) collective-permute-start(bf16[2,1024,128]{1,2,0:T(8,128)(2,1)} %pad_maximum_fusion.1), channel_id=1, source_target_pairs={{0,16},{16,0},{32,48},{48,32},{64,80},{80,64},{96,112},{112,96},{1... | collective-permute-start | bytes 1572872 | tf_op jit(solution)/shard_map/ppermute | solution.py:21
  152.2 12.2 %copy-start.3 = (bf16[1024,128]{0,1:T(8,128)(2,1)S(1)}, bf16[1024,128]{0,1:T(8,128)(2,1)}, u32[]{:S(2)}) copy-start(bf16[1024,128]{0,1:T(8,128)(2,1)} %get-tuple-element.109) | copy-start | bytes 786436
  172.3 3.9 %copy-start.4 = (bf16[2048,128]{1,0:T(8,128)(2,1)S(1)}, bf16[2048,128]{1,0:T(8,128)(2,1)}, u32[]{:S(2)}) copy-start(bf16[2048,128]{1,0:T(8,128)(2,1)} %get-tuple-element.210) | copy-start | bytes 1572868 | tf_op jit(solution)/shard_map/while
  181.9 3.9 %copy-start.4 = (bf16[2048,128]{1,0:T(8,128)(2,1)S(1)}, bf16[2048,128]{1,0:T(8,128)(2,1)}, u32[]{:S(2)}) copy-start(bf16[2048,128]{1,0:T(8,128)(2,1)} %get-tuple-element.210) | copy-start | bytes 1572868 | tf_op jit(solution)/shard_map/while
  213.9 4.6 %copy-start.7 = (s32[64,8]{0,1:T(8,128)S(1)}, s32[64,8]{0,1:T(8,128)}, u32[]{:S(2)}) copy-start(s32[64,8]{0,1:T(8,128)} %param.27) | copy-start | bytes 6148
  218.5 65.6 %copy-start.1 = (bf16[64,2048]{1,0:T(8,128)(2,1)S(1)}, bf16[64,2048]{1,0:T(8,128)(2,1)}, u32[]{:S(2)}) copy-start(bf16[64,2048]{1,0:T(8,128)(2,1)} %param.15) | copy-start | bytes 786436
  218.5 67.5 %copy-start.6 = (f32[2048]{0:T(1024)S(1)}, f32[2048]{0:T(1024)}, u32[]{:S(2)}) copy-start(f32[2048]{0:T(1024)} %param.17) | copy-start | bytes 24580
  285.3 0.7 copy-start.2
  287.1 14.8 %all-to-all-start.1 = ((bf16[16,4,2048]{2,1,0:T(4,128)(2,1)}), bf16[16,4,2048]{2,1,0:T(4,128)(2,1)S(1)}, u32[]{:S(2)}, u32[]{:S(2)}) async-start(bf16[16,4,2048]{2,1,0:T(4,128)(2,1)} %reshape.270), calls=%async_computation.2 | async-start | bytes 524288 | tf_op jit(solution)/shard_map/all_to_all | solution.py:180
  308.1 12.3 %all-to-all-start.2 = ((bf16[16,4,2048]{2,1,0:T(4,128)(2,1)}), bf16[16,4,2048]{2,1,0:T(4,128)(2,1)}, u32[]{:S(2)}, u32[]{:S(2)}) async-start(bf16[16,4,2048]{2,1,0:T(4,128)(2,1)} %reshape.272), calls=%async_computation.3 | async-start | bytes 524288 | tf_op jit(solution)/shard_map/all_to_all | solution.py:191
Sparse Core Ops, SparseCore 0:
  10.6 84.6 all-gather.5
  97.7 40.6 all-gather.3
  141.4 72.4 all-gather.7
  218.6 65.4 reduce-scatter.1
